TPU v7x, 32 devices: a whole 2x2x4 slice. The times are simulated.
32 devices in a mesh: cuts: 2 (over y), group: 16 (over z, x, core).
Axes of the slice: x: 2, y: 2, z: 4, core: 2. Of those that a mesh axis runs over, the one named last changes fastest.
Arguments:
- stem_blocks: bfloat16 [2, 64, 1024, 512], P('cuts', None, 'group'), may hold values from -6 to 6
- cap_tensor: bfloat16 [2, 2, 256, 256], P('cuts'), may hold values from -0.1875 to 0.1875
- slot_rows: int32 [64, 1024], P('group'), may hold values from 0 to 1023
- counts: int32 [64], P('group'), may hold values from 128 to 1024, as said below
Outputs:
- amplitudes: bfloat16 [1024, 64, 512], P('cuts', 'group')
Inputs may be any that keep to these rules, and one draw needn't show every extreme that they name: `counts`: some group has exactly 1024 live slots in every draw.
All inputs are finite; a program needn't handle non-finite values.
Results may differ from a plain program's by a relative error of at most 0.0052.
Values may be sent and summed in bfloat16 or wider, within the bound.
No kernel may reach another device: no remote copies, remote signals or barrier semaphores. Data moves between devices by JAX's collectives and lax.ppermute only.
A program may use at most 64 MiB of HBM per device.

v0:
```python
import jax
import jax.numpy as jnp
from jax import lax
from jax.sharding import PartitionSpec as P


def build_matrix(cap_pair):
    real_part = cap_pair[0]
    imag_part = cap_pair[1]
    upper = jnp.concatenate([real_part, imag_part], axis=1)
    lower = jnp.concatenate([-imag_part, real_part], axis=1)
    return jnp.concatenate([upper, lower], axis=0)


def local(stem_blocks, cap_tensor, slot_rows, counts):
    owned_rows = lax.all_to_all(stem_blocks[0], "group", split_axis=0, concat_axis=1, tiled=True)
    matrix = build_matrix(cap_tensor[0])
    slot_total = slot_rows.shape[1]
    share = slot_total // lax.axis_size("cuts")
    positions = jnp.arange(slot_total, dtype=jnp.int32)
    live_mask = positions[None, :] < counts[:, None]
    picked = jnp.take_along_axis(owned_rows, slot_rows[:, :, None], axis=1)
    product = jnp.einsum("gcr,rs->cgs", picked, matrix, preferred_element_type=jnp.float32)
    whole_sum = lax.psum(
        jnp.where(jnp.transpose(live_mask)[:, :, None], product, jnp.float32(0.0)).astype(
            jnp.bfloat16
        ),
        "cuts",
    ).astype(jnp.float32)
    summed = lax.dynamic_slice_in_dim(whole_sum, lax.axis_index("cuts") * share, share, 0)
    return summed.astype(jnp.bfloat16)


def solution(mesh):
    in_specs = (
        P("cuts", None, "group", None),
        P("cuts", None, None, None),
        P("group", None),
        P("group"),
    )
    out_specs = P("cuts", "group", None)
    return jax.shard_map(local, mesh=mesh, in_specs=in_specs, out_specs=out_specs, check_vma=False)
```

profile of v0, /device:TPU:0, one launch (start us, length us, event | category | flops | bytes accessed | tf_op | source)
XLA Modules:
  0.0 309.5 jit_solution(17406738748968861879)
XLA Ops:
  6.5 0.0 copy-start.1
  6.5 0.0 copy-start
  6.5 0.0 copy-start.2
  6.5 7.5 %all-to-all-start = ((bf16[64,64,512]{2,1,0:T(8,128)(2,1)}), bf16[64,64,512]{2,1,0:T(8,128)(2,1)}, u32[]{:S(2)}, u32[]{:S(2)}) async-start(bf16[64,64,512]{2,1,0:T(8,128)(2,1)} %bitcast.29), calls=%async_computation | async-start | bytes 8388608 | tf_op jit(solution)/shard_map/all_to_all | solution.py:16
  14.1 0.0 all-reduce.2.cloned.1.call-start
  14.1 0.0 copy-done.1
  14.2 0.0 copy-done
  14.2 0.1 copy.9
  14.3 0.1 copy.10
  14.4 0.0 copy-done.2
  14.4 0.1 iota_compare_fusion
  14.6 77.2 %all-to-all-done = bf16[64,64,512]{2,1,0:T(8,128)(2,1)} async-done(((bf16[64,64,512]{2,1,0:T(8,128)(2,1)}), bf16[64,64,512]{2,1,0:T(8,128)(2,1)}, u32[]{:S(2)}, u32[]{:S(2)}) %all-to-all-start) | async-done | bytes 4194336 | tf_op jit(solution)/shard_map/all_to_all | solution.py:16
  91.8 4.6 %copy.7 = bf16[16,4,64,512]{3,2,0,1:T(8,128)(2,1)} copy(bf16[16,4,64,512]{3,2,1,0:T(8,128)(2,1)} %bitcast.4) | data formatting | bytes 8388608 | tf_op jit(solution)/shard_map/all_to_all | solution.py:16
  96.4 72.6 %gather_fusion = bf16[4096,512]{1,0:T(8,128)(2,1)} fusion(bf16[4,1024,512]{2,1,0:T(8,128)(2,1)} %bitcast.26, s32[4096]{0:T(1024)S(1)} %bitcast.27), kind=kCustom, calls=%fused_computation | custom fusion | bytes 8421376 | tf_op jit(solution)/shard_map/jit(take_along_axis)/gather | solution.py:22
  169.0 5.8 %fusion = bf16[1024,4,512]{0,2,1:T(8,128)(2,1)} fusion(pred[1024,4]{0,1:T(4,128)(4,1)S(1)} %iota_compare_fusion, bf16[4,1024,512]{2,1,0:T(8,128)(2,1)} %bitcast.28, pred[4,1024]{1,0:T(4,128)(4,1)S(1)} %compare_and_fusion, bf16[256,256]{0,1:T(8,128)(2,1)S(1)} %bitcast.31, bf16[256,256]{0,1:T(8,128)(2,1)S(1)} %bitcast_negate_fusion, ...), kind=kOutput, calls=%fused_computation.2 | convolution fusion | flops 2155872256 | bytes 8790016 | tf_op jit(solution)/shard_map/gcr,rs->cgs/dot_general | solution.py:23
  174.8 0.0 all-reduce.2.cloned.1.call-update
  174.9 123.0 %all-reduce.2.cloned.1.call-done = bf16[1024,4,512]{0,2,1:T(8,128)(2,1)} async-done(((bf16[1024,4,512]{0,2,1:T(8,128)(2,1)}), bf16[1024,4,512]{0,2,1:T(8,128)(2,1)}) %all-reduce.2.cloned.1.call-update) | async-done | bytes 4194320 | tf_op jit(solution)/shard_map/psum | solution.py:24
  297.9 1.7 convert_convert_fusion
  299.6 3.1 copy.8
  (5 shorter events, 0.1 us)
Async XLA Ops:
  6.5 7.6 %copy-start.1 = (s32[4,1024]{1,0:T(4,128)S(1)}, s32[4,1024]{1,0:T(4,128)}, u32[]{:S(2)}) copy-start(s32[4,1024]{1,0:T(4,128)} %param.6) | copy-start | bytes 49156
  6.5 7.6 %copy-start = (bf16[1,2,256,256]{3,2,1,0:T(8,128)(2,1)S(1)}, bf16[1,2,256,256]{3,2,1,0:T(8,128)(2,1)}, u32[]{:S(2)}) copy-start(bf16[1,2,256,256]{3,2,1,0:T(8,128)(2,1)} %param.5) | copy-start | bytes 786436
  6.5 7.9 %copy-start.2 = (s32[4]{0:T(128)S(1)}, s32[4]{0:T(128)}, u32[]{:S(2)}) copy-start(s32[4]{0:T(128)} %param.7) | copy-start | bytes 52
  6.5 85.2 %all-to-all-start = ((bf16[64,64,512]{2,1,0:T(8,128)(2,1)}), bf16[64,64,512]{2,1,0:T(8,128)(2,1)}, u32[]{:S(2)}, u32[]{:S(2)}) async-start(bf16[64,64,512]{2,1,0:T(8,128)(2,1)} %bitcast.29), calls=%async_computation | async-start | bytes 8388608 | tf_op jit(solution)/shard_map/all_to_all | solution.py:16
  14.1 283.8 %all-reduce.2.cloned.1.call-start = ((), (), s32[]{:S(2)}) async-start(), calls=%async_computation.1 | async-start | bytes 8388608 | tf_op jit(solution)/shard_map/psum | solution.py:24
Sparse Core Ops, SparseCore 0:
  175.0 122.8 all-reduce.1
where the time goes:
time: 311 us; the launch traced here: 310 us
  waiting for transfers between devices  200 us (64%)
  local copies, waits for them, and re-layouts  80.5 us (26%)
  between operations  13.5 us (4%)
  starting transfers between devices  7.58 us (2%)
  matrix products  5.84 us (2%)
    psum x1, waiting for transfers between devices, local(): lax.psum(jnp.where(jnp.transpose(live_mask)[:, :, None], product, jnp.flo...  123 us
    all_to_all x1, waiting for transfers between devices, local(): lax.all_to_all(stem_blocks[0], 'group', split_axis=0, concat_axis=1, tile...  77.2 us
    gather x1, local copies, waits for them, and re-layouts, local(): picked = jnp.take_along_axis(owned_rows, slot_rows[:, :, None], axis=1)  72.6 us
    all_to_all x1, starting transfers between devices, local(): lax.all_to_all(stem_blocks[0], 'group', split_axis=0, concat_axis=1, tile...  7.54 us
  transfers between devices with their start and end apart: 2, of which 2 were waited for; matrix products, arithmetic and copies ran while one was open for 0% of the time, Pallas kernels for 0%

commit v1 on v0

--- a/solution.py
+++ b/solution.py
@@ -21,11 +21,14 @@
     live_mask = positions[None, :] < counts[:, None]
     picked = jnp.take_along_axis(owned_rows, slot_rows[:, :, None], axis=1)
     product = jnp.einsum("gcr,rs->cgs", picked, matrix, preferred_element_type=jnp.float32)
-    whole_sum = lax.psum(
-        jnp.where(jnp.transpose(live_mask)[:, :, None], product, jnp.float32(0.0)).astype(
-            jnp.bfloat16
+    whole_sum = jnp.sum(
+        lax.all_gather(
+            jnp.where(jnp.transpose(live_mask)[:, :, None], product, jnp.float32(0.0)).astype(
+                jnp.bfloat16
+            ),
+            "cuts",
         ),
-        "cuts",
+        axis=0,
     ).astype(jnp.float32)
     summed = lax.dynamic_slice_in_dim(whole_sum, lax.axis_index("cuts") * share, share, 0)
     return summed.astype(jnp.bfloat16)

time: 311 us -> 345 us (1.11)
  other arithmetic: 1.84 us -> 25.6 us
  local copies, waits for them, and re-layouts: 80.5 us -> 95 us
  waiting for transfers between devices: 200 us -> 196 us
    psum x1 -> x0, waiting for transfers between devices: 123 us -> none  [local(): lax.psum(jnp.where(jnp.transpose(live_mask)[:, :, None], product, jnp.flo...]
    all_gather x0 -> x1, waiting for transfers between devices: none -> 119 us  [local(): lax.all_gather(jnp.where(jnp.transpose(live_mask)[:, :, None], product, j...]
    reduce_sum x0 -> x1, other arithmetic: none -> 23.8 us  [local(): jnp.sum(lax.all_gather(jnp.where(jnp.transpose(live_mask)[:, :, None], pr...]
    all_gather x0 -> x1, local copies, waits for them, and re-layouts: none -> 14.5 us  [local(): lax.all_gather(jnp.where(jnp.transpose(live_mask)[:, :, None], product, j...]
where the time goes in v1:
time: 345 us; the launch traced here: 344 us
  waiting for transfers between devices  196 us (57%)
  local copies, waits for them, and re-layouts  95 us (28%)
  other arithmetic  25.6 us (7%)
  between operations  13.5 us (4%)
  starting transfers between devices  7.58 us (2%)
  matrix products  5.77 us (2%)
    all_gather x1, waiting for transfers between devices, local(): lax.all_gather(jnp.where(jnp.transpose(live_mask)[:, :, None], product, j...  119 us
    all_to_all x1, waiting for transfers between devices, local(): lax.all_to_all(stem_blocks[0], 'group', split_axis=0, concat_axis=1, tile...  77.2 us
    gather x1, local copies, waits for them, and re-layouts, local(): picked = jnp.take_along_axis(owned_rows, slot_rows[:, :, None], axis=1)  72.6 us
    reduce_sum x1, other arithmetic, local(): jnp.sum(lax.all_gather(jnp.where(jnp.transpose(live_mask)[:, :, None], pr...  23.8 us
    all_gather x1, local copies, waits for them, and re-layouts, local(): lax.all_gather(jnp.where(jnp.transpose(live_mask)[:, :, None], product, j...  14.5 us
    all_to_all x1, starting transfers between devices, local(): lax.all_to_all(stem_blocks[0], 'group', split_axis=0, concat_axis=1, tile...  7.54 us
  transfers between devices with their start and end apart: 2, of which 2 were waited for; matrix products, arithmetic and copies ran while one was open for 0% of the time, Pallas kernels for 0%

profile of v1, /device:TPU:0, one launch (start us, length us, event | category | flops | bytes accessed | tf_op | source)
XLA Modules:
  0.0 343.9 jit_solution(17121655279956932710)
XLA Ops:
  6.5 0.0 copy-start.1
  6.5 0.0 copy-start
  6.5 0.0 copy-start.2
  6.5 7.5 %all-to-all-start = ((bf16[64,64,512]{2,1,0:T(8,128)(2,1)}), bf16[64,64,512]{2,1,0:T(8,128)(2,1)}, u32[]{:S(2)}, u32[]{:S(2)}) async-start(bf16[64,64,512]{2,1,0:T(8,128)(2,1)} %bitcast.31), calls=%async_computation | async-start | bytes 8388608 | tf_op jit(solution)/shard_map/all_to_all | solution.py:16
  14.1 0.0 all-gather.3.cloned.1.call-start
  14.1 0.0 copy-done.1
  14.2 0.0 copy-done
  14.2 0.1 copy.12
  14.3 0.1 copy.13
  14.4 0.0 copy-done.2
  14.4 0.1 iota_compare_fusion
  14.6 77.2 %all-to-all-done = bf16[64,64,512]{2,1,0:T(8,128)(2,1)} async-done(((bf16[64,64,512]{2,1,0:T(8,128)(2,1)}), bf16[64,64,512]{2,1,0:T(8,128)(2,1)}, u32[]{:S(2)}, u32[]{:S(2)}) %all-to-all-start) | async-done | bytes 4194336 | tf_op jit(solution)/shard_map/all_to_all | solution.py:16
  91.8 4.6 %copy.10 = bf16[16,4,64,512]{3,2,0,1:T(8,128)(2,1)} copy(bf16[16,4,64,512]{3,2,1,0:T(8,128)(2,1)} %bitcast.4) | data formatting | bytes 8388608 | tf_op jit(solution)/shard_map/all_to_all | solution.py:16
  96.4 72.6 %gather_fusion = bf16[4096,512]{1,0:T(8,128)(2,1)} fusion(bf16[4,1024,512]{2,1,0:T(8,128)(2,1)} %bitcast.28, s32[4096]{0:T(1024)S(1)} %bitcast.29), kind=kCustom, calls=%fused_computation | custom fusion | bytes 8421376 | tf_op jit(solution)/shard_map/jit(take_along_axis)/gather | solution.py:22
  169.0 5.8 %fusion = bf16[1024,4,512]{0,2,1:T(8,128)(2,1)} fusion(pred[1024,4]{0,1:T(4,128)(4,1)S(1)} %iota_compare_fusion, bf16[4,1024,512]{2,1,0:T(8,128)(2,1)} %bitcast.30, pred[4,1024]{1,0:T(4,128)(4,1)S(1)} %compare_and_fusion, bf16[256,256]{0,1:T(8,128)(2,1)S(1)} %bitcast.33, bf16[256,256]{0,1:T(8,128)(2,1)S(1)} %bitcast_negate_fusion, ...), kind=kOutput, calls=%fused_computation.2 | convolution fusion | flops 2155872256 | bytes 8790016 | tf_op jit(solution)/shard_map/gcr,rs->cgs/dot_general | solution.py:23
  174.8 0.0 all-gather.3.cloned.1.call-update
  174.8 119.2 %all-gather.3.cloned.1.call-done = bf16[2048,4,512]{0,2,1:T(8,128)(2,1)} async-done(((bf16[1024,4,512]{0,2,1:T(8,128)(2,1)}), bf16[2048,4,512]{0,2,1:T(8,128)(2,1)}) %all-gather.3.cloned.1.call-update) | async-done | bytes 8388624 | tf_op jit(solution)/shard_map/all_gather | solution.py:25
  294.0 14.5 %reshape.36 = bf16[2,1024,4,512]{1,0,3,2:T(2,128)(2,1)} reshape(bf16[2048,4,512]{0,2,1:T(8,128)(2,1)} %all-gather.3.cloned.1.call-done) | data formatting | bytes 16777216 | tf_op jit(solution)/shard_map/all_gather | solution.py:25
  308.5 23.8 %reduce_sum.12 = bf16[1024,4,512]{0,2,1:T(8,128)(2,1)} reduce(bf16[2,1024,4,512]{1,0,3,2:T(2,128)(2,1)} %reshape.36, bf16[]{:T(256)} %constant.24.clone.1), dimensions={0}, to_apply=%region_0.0 | reduce | flops 2097152 | bytes 12582914 | tf_op jit(solution)/shard_map/reduce_sum | solution.py:24
  332.3 1.7 convert_convert_fusion
  334.0 3.1 copy.11
  (5 shorter events, 0.1 us)
Async XLA Ops:
  6.5 7.6 %copy-start.1 = (s32[4,1024]{1,0:T(4,128)S(1)}, s32[4,1024]{1,0:T(4,128)}, u32[]{:S(2)}) copy-start(s32[4,1024]{1,0:T(4,128)} %param.6) | copy-start | bytes 49156
  6.5 7.6 %copy-start = (bf16[1,2,256,256]{3,2,1,0:T(8,128)(2,1)S(1)}, bf16[1,2,256,256]{3,2,1,0:T(8,128)(2,1)}, u32[]{:S(2)}) copy-start(bf16[1,2,256,256]{3,2,1,0:T(8,128)(2,1)} %param.5) | copy-start | bytes 786436
  6.5 7.9 %copy-start.2 = (s32[4]{0:T(128)S(1)}, s32[4]{0:T(128)}, u32[]{:S(2)}) copy-start(s32[4]{0:T(128)} %param.7) | copy-start | bytes 52
  6.5 85.2 %all-to-all-start = ((bf16[64,64,512]{2,1,0:T(8,128)(2,1)}), bf16[64,64,512]{2,1,0:T(8,128)(2,1)}, u32[]{:S(2)}, u32[]{:S(2)}) async-start(bf16[64,64,512]{2,1,0:T(8,128)(2,1)} %bitcast.31), calls=%async_computation | async-start | bytes 8388608 | tf_op jit(solution)/shard_map/all_to_all | solution.py:16
  14.1 279.9 %all-gather.3.cloned.1.call-start = ((), (), s32[]{:S(2)}) async-start(), calls=%async_computation.1 | async-start | bytes 12582912 | tf_op jit(solution)/shard_map/all_gather | solution.py:25
Sparse Core Ops, SparseCore 0:
  174.9 119.0 all-gather.2
